TPU v7x, 32 devices: a whole 2x2x4 slice. The times are simulated.
32 devices in a mesh: mode: 8 (over y, x, core), rows: 4 (over z).
Axes of the slice: x: 2, y: 2, z: 4, core: 2. Of those that a mesh axis runs over, the one named last changes fastest.
Arguments:
- tangents: float32 [128, 3, 32, 1024], P('mode', None, 'rows'), may hold values from -6 to 6
- checkpoints: float32 [8, 3, 32, 1024], P(None, None, 'rows', 'mode'), may hold values from 0 to 0.5
- owner_order: int32 [8], replicated, may hold values from 0 to 7, each once
- land_mask: int32 [32, 1024], P('rows'), may hold values 0 or 1
- coefficients: float32 [128, 128], replicated, may hold values from -0.9 to 0.9
Outputs:
- vectors: float32 [128, 3, 32, 1024], P(None, None, 'rows', 'mode')
Inputs may be any that keep to these rules, and one draw needn't show every extreme that they name: `owner_order`: every checkpoint slot is named by exactly one step.
All inputs are finite; a program needn't handle non-finite values. No bound on the sum of `land_mask` on one device may be relied on, other than what follows from the above.
Results may differ from a plain program's by a relative error of at most 0.0002.
Values sent between devices are 32-bit elements; how exact they have to be, the bound alone decides.
A program may use at most 64 MiB of HBM per device.

v0:
```python
import jax
import jax.numpy as jnp
from jax import lax
from jax.sharding import PartitionSpec as P

mean_depth = 1.0
gravity = 1.0
coriolis = 0.5
time_step = 0.5


def padded(cells, sides, width):
    for axis, dim in sides:
        count = lax.axis_size(axis)
        ends = count - 1
        head = lax.slice_in_dim(cells, 0, width, axis=dim)
        tail = lax.slice_in_dim(cells, cells.shape[dim] - width, cells.shape[dim], axis=dim)
        cells = jnp.concatenate(
            [
                lax.ppermute(tail, axis, [(i, (i + 1) % count) for i in range(ends)]),
                cells,
                lax.ppermute(head, axis, [((i + 1) % count, i) for i in range(ends)]),
            ],
            axis=dim,
        )
    return cells


def deriv_x(values):
    return 0.5 * (jnp.roll(values, -1, -1) - jnp.roll(values, 1, -1))


def deriv_y(values):
    return 0.5 * (values[..., 2:, :] - values[..., :-2, :])


def interior(values):
    return values[..., 1:-1, :]


def tendency(base_flow, current):
    depth_total = mean_depth + base_flow[0]
    flow_u = base_flow[1]
    flow_v = base_flow[2]
    height = current[:, 0]
    zonal = current[:, 1]
    meridional = current[:, 2]
    flux_x = depth_total * zonal + height * flow_u
    flux_y = depth_total * meridional + height * flow_v
    height_rate = -(interior(deriv_x(flux_x)) + deriv_y(flux_y))
    zonal_mid = interior(zonal)
    merid_mid = interior(meridional)
    flow_umid = interior(flow_u)
    flow_vmid = interior(flow_v)
    zonal_rate = (
        -(
            flow_umid * interior(deriv_x(zonal))
            + zonal_mid * interior(deriv_x(flow_u))
            + flow_vmid * deriv_y(zonal)
            + merid_mid * deriv_y(flow_u)
        )
        + coriolis * merid_mid
        - gravity * interior(deriv_x(height))
    )
    merid_rate = (
        -(
            flow_umid * interior(deriv_x(meridional))
            + zonal_mid * interior(deriv_x(flow_v))
            + flow_vmid * deriv_y(meridional)
            + merid_mid * deriv_y(flow_v)
        )
        - coriolis * zonal_mid
        - gravity * deriv_y(height)
    )
    return jnp.stack([height_rate, zonal_rate, merid_rate], 1)


def step_wide(base_wide, state_wide, wet_wide):
    slope_one = tendency(base_wide, state_wide)
    middle = wet_wide[1:-1] * (state_wide[:, :, 1:-1] + time_step * slope_one)
    slope_two = tendency(base_wide[:, 1:-1], middle)
    return wet_wide[2:-2] * (
        state_wide[:, :, 2:-2] + 0.5 * time_step * (slope_one[:, :, 1:-1] + slope_two)
    )


def on_device(tangents, checkpoints, owner_order, land_mask, coefficients):
    wet_mask = land_mask.astype(jnp.float32)
    current = wet_mask * tangents
    depth = 2
    flows_wide, wet_stack = (
        padded(checkpoints, (("rows", 2),), depth),
        padded(wet_mask[None, None], (("rows", 2),), depth),
    )
    wet_wide = wet_stack[0, 0]

    def fetch_flow(step_index):
        held_tile = lax.dynamic_index_in_dim(flows_wide, owner_order[step_index], 0, keepdims=False)
        return lax.all_gather(held_tile, "mode", axis=2, tiled=True)

    total_steps = owner_order.shape[0]

    def advance(step_index, current):
        widened = padded(current, (("rows", 2),), 2)
        return step_wide(fetch_flow(step_index), widened, wet_wide)

    final = lax.fori_loop(0, total_steps, advance, current)
    mixing = jnp.eye(coefficients.shape[0], dtype=jnp.float32) + jnp.triu(coefficients)
    cell_block = lax.all_to_all(final, "mode", split_axis=3, concat_axis=0, tiled=True)
    flattened = cell_block.reshape(cell_block.shape[0], -1)
    mixed = jnp.dot(
        mixing.T, flattened, precision=lax.Precision.HIGHEST, preferred_element_type=jnp.float32
    )
    return mixed.reshape(cell_block.shape)


def solution(mesh):
    placed = (
        P("mode", None, "rows", None),
        P(None, None, "rows", "mode"),
        P(),
        P("rows", None),
        P(),
    )
    return jax.shard_map(
        on_device,
        mesh=mesh,
        in_specs=placed,
        out_specs=P(None, None, "rows", "mode"),
        check_vma=False,
    )
```

profile of v0, /device:TPU:0, one launch (start us, length us, event | category | flops | bytes accessed | tf_op | source)
XLA Modules:
  0.0 402.4 jit_solution(8135360196230346554)
XLA Ops:
  1.0 5.0 %collective-permute-start.4 = (f32[8,3,2,128]{3,2,1,0:T(2,128)S(1)}, f32[8,3,2,128]{3,2,1,0:T(2,128)S(1)}, u32[]{:S(2)}, u32[]{:S(2)}) collective-permute-start(f32[8,3,2,128]{3,2,1,0:T(2,128)S(1)} %get-tuple-element.196), channel_id=1, source_target_pairs={{0,1},{1,2},{2,3},{4,5},{5,6},{6,7},{8,9},{9,10},{10,11},{12,13},{... | collective-permute-start | bytes 73736 | tf_op jit(solution)/shard_map/ppermute | solution.py:20
  8.0 4.5 %collective-permute-start.2 = (f32[1,1,2,1024]{3,2,1,0:T(2,128)S(1)}, f32[1,1,2,1024]{3,2,1,0:T(2,128)S(1)}, u32[]{:S(2)}, u32[]{:S(2)}) collective-permute-start(f32[1,1,2,1024]{3,2,1,0:T(2,128)S(1)} %get-tuple-element.198), channel_id=1, source_target_pairs={{0,1},{1,2},{2,3},{4,5},{5,6},{6,7},{8,9},{9,10},{10,11},{12,13},{... | collective-permute-start | bytes 24584 | tf_op jit(solution)/shard_map/ppermute | solution.py:20
  18.8 316.0 %while.13 = (s32[]{:T(128)}, f32[16,3,8,1024]{3,2,1,0:T(8,128)S(1)}, f32[12,1024]{1,0:T(8,128)}, s32[8]{0:T(128)S(1)}, f32[8,3,12,128]{3,2,1,0:T(8,128)S(1)}, /*...) while((s32[]{:T(128)}, f32[16,3,8,1024]{3,2,1,0:T(8,128)S(1)}, f32[12,1024]{1,0:T(8,128)}, s32[8]{0:T(128)S(1)}, ...), condition=%wide.region_1.2_spmd, body=%wide.region_0.1_spmd.sunk | while | flops 21987332 | bytes 97589864 | solution.py:107
  20.5 5.3 %collective-permute-start.1 = (f32[16,3,2,1024]{3,2,0,1:T(2,128)S(1)}, f32[16,3,2,1024]{3,2,0,1:T(2,128)}, u32[]{:S(2)}, u32[]{:S(2)}) collective-permute-start(f32[16,3,2,1024]{3,2,0,1:T(2,128)S(1)} %get-tuple-element.308), channel_id=1, source_target_pairs={{0,1},{1,2},{2,3},{4,5},{5,6},{6,7},{8,9},{9,10},{10,11},{12,13},{... | collective-permute-start | bytes 1179656 | tf_op jit(solution)/shard_map/while/body/eval_jaxpr/ppermute | solution.py:20
  28.5 9.6 %all-gather.2 = f32[1,3,12,1024]{3,2,1,0:T(8,128)S(1)} all-gather(f32[1,3,12,128]{3,2,1,0:T(8,128)S(1)} %constant_dynamic-slice_fusion.2), channel_id=2, replica_groups=mesh['mode'=8,'rows'=4] {'mode'}, dimensions={3}, use_global_device_ids=true | all-gather | bytes 165888 | tf_op jit(solution)/shard_map/while/body/eval_jaxpr/all_gather | solution.py:99
  60.3 5.3 %collective-permute-start.1 = (f32[16,3,2,1024]{3,2,0,1:T(2,128)S(1)}, f32[16,3,2,1024]{3,2,0,1:T(2,128)}, u32[]{:S(2)}, u32[]{:S(2)}) collective-permute-start(f32[16,3,2,1024]{3,2,0,1:T(2,128)S(1)} %get-tuple-element.308), channel_id=1, source_target_pairs={{0,1},{1,2},{2,3},{4,5},{5,6},{6,7},{8,9},{9,10},{10,11},{12,13},{... | collective-permute-start | bytes 1179656 | tf_op jit(solution)/shard_map/while/body/eval_jaxpr/ppermute | solution.py:20
  68.4 9.6 %all-gather.2 = f32[1,3,12,1024]{3,2,1,0:T(8,128)S(1)} all-gather(f32[1,3,12,128]{3,2,1,0:T(8,128)S(1)} %constant_dynamic-slice_fusion.2), channel_id=2, replica_groups=mesh['mode'=8,'rows'=4] {'mode'}, dimensions={3}, use_global_device_ids=true | all-gather | bytes 165888 | tf_op jit(solution)/shard_map/while/body/eval_jaxpr/all_gather | solution.py:99
  100.2 5.3 %collective-permute-start.1 = (f32[16,3,2,1024]{3,2,0,1:T(2,128)S(1)}, f32[16,3,2,1024]{3,2,0,1:T(2,128)}, u32[]{:S(2)}, u32[]{:S(2)}) collective-permute-start(f32[16,3,2,1024]{3,2,0,1:T(2,128)S(1)} %get-tuple-element.308), channel_id=1, source_target_pairs={{0,1},{1,2},{2,3},{4,5},{5,6},{6,7},{8,9},{9,10},{10,11},{12,13},{... | collective-permute-start | bytes 1179656 | tf_op jit(solution)/shard_map/while/body/eval_jaxpr/ppermute | solution.py:20
  108.2 8.6 %all-gather.2 = f32[1,3,12,1024]{3,2,1,0:T(8,128)S(1)} all-gather(f32[1,3,12,128]{3,2,1,0:T(8,128)S(1)} %constant_dynamic-slice_fusion.2), channel_id=2, replica_groups=mesh['mode'=8,'rows'=4] {'mode'}, dimensions={3}, use_global_device_ids=true | all-gather | bytes 165888 | tf_op jit(solution)/shard_map/while/body/eval_jaxpr/all_gather | solution.py:99
  139.0 5.3 %collective-permute-start.1 = (f32[16,3,2,1024]{3,2,0,1:T(2,128)S(1)}, f32[16,3,2,1024]{3,2,0,1:T(2,128)}, u32[]{:S(2)}, u32[]{:S(2)}) collective-permute-start(f32[16,3,2,1024]{3,2,0,1:T(2,128)S(1)} %get-tuple-element.308), channel_id=1, source_target_pairs={{0,1},{1,2},{2,3},{4,5},{5,6},{6,7},{8,9},{9,10},{10,11},{12,13},{... | collective-permute-start | bytes 1179656 | tf_op jit(solution)/shard_map/while/body/eval_jaxpr/ppermute | solution.py:20
  147.1 9.6 %all-gather.2 = f32[1,3,12,1024]{3,2,1,0:T(8,128)S(1)} all-gather(f32[1,3,12,128]{3,2,1,0:T(8,128)S(1)} %constant_dynamic-slice_fusion.2), channel_id=2, replica_groups=mesh['mode'=8,'rows'=4] {'mode'}, dimensions={3}, use_global_device_ids=true | all-gather | bytes 165888 | tf_op jit(solution)/shard_map/while/body/eval_jaxpr/all_gather | solution.py:99
  178.9 5.3 %collective-permute-start.1 = (f32[16,3,2,1024]{3,2,0,1:T(2,128)S(1)}, f32[16,3,2,1024]{3,2,0,1:T(2,128)}, u32[]{:S(2)}, u32[]{:S(2)}) collective-permute-start(f32[16,3,2,1024]{3,2,0,1:T(2,128)S(1)} %get-tuple-element.308), channel_id=1, source_target_pairs={{0,1},{1,2},{2,3},{4,5},{5,6},{6,7},{8,9},{9,10},{10,11},{12,13},{... | collective-permute-start | bytes 1179656 | tf_op jit(solution)/shard_map/while/body/eval_jaxpr/ppermute | solution.py:20
  186.9 8.6 %all-gather.2 = f32[1,3,12,1024]{3,2,1,0:T(8,128)S(1)} all-gather(f32[1,3,12,128]{3,2,1,0:T(8,128)S(1)} %constant_dynamic-slice_fusion.2), channel_id=2, replica_groups=mesh['mode'=8,'rows'=4] {'mode'}, dimensions={3}, use_global_device_ids=true | all-gather | bytes 165888 | tf_op jit(solution)/shard_map/while/body/eval_jaxpr/all_gather | solution.py:99
  217.8 5.3 %collective-permute-start.1 = (f32[16,3,2,1024]{3,2,0,1:T(2,128)S(1)}, f32[16,3,2,1024]{3,2,0,1:T(2,128)}, u32[]{:S(2)}, u32[]{:S(2)}) collective-permute-start(f32[16,3,2,1024]{3,2,0,1:T(2,128)S(1)} %get-tuple-element.308), channel_id=1, source_target_pairs={{0,1},{1,2},{2,3},{4,5},{5,6},{6,7},{8,9},{9,10},{10,11},{12,13},{... | collective-permute-start | bytes 1179656 | tf_op jit(solution)/shard_map/while/body/eval_jaxpr/ppermute | solution.py:20
  225.8 9.6 %all-gather.2 = f32[1,3,12,1024]{3,2,1,0:T(8,128)S(1)} all-gather(f32[1,3,12,128]{3,2,1,0:T(8,128)S(1)} %constant_dynamic-slice_fusion.2), channel_id=2, replica_groups=mesh['mode'=8,'rows'=4] {'mode'}, dimensions={3}, use_global_device_ids=true | all-gather | bytes 165888 | tf_op jit(solution)/shard_map/while/body/eval_jaxpr/all_gather | solution.py:99
  257.6 5.3 %collective-permute-start.1 = (f32[16,3,2,1024]{3,2,0,1:T(2,128)S(1)}, f32[16,3,2,1024]{3,2,0,1:T(2,128)}, u32[]{:S(2)}, u32[]{:S(2)}) collective-permute-start(f32[16,3,2,1024]{3,2,0,1:T(2,128)S(1)} %get-tuple-element.308), channel_id=1, source_target_pairs={{0,1},{1,2},{2,3},{4,5},{5,6},{6,7},{8,9},{9,10},{10,11},{12,13},{... | collective-permute-start | bytes 1179656 | tf_op jit(solution)/shard_map/while/body/eval_jaxpr/ppermute | solution.py:20
  265.6 8.6 %all-gather.2 = f32[1,3,12,1024]{3,2,1,0:T(8,128)S(1)} all-gather(f32[1,3,12,128]{3,2,1,0:T(8,128)S(1)} %constant_dynamic-slice_fusion.2), channel_id=2, replica_groups=mesh['mode'=8,'rows'=4] {'mode'}, dimensions={3}, use_global_device_ids=true | all-gather | bytes 165888 | tf_op jit(solution)/shard_map/while/body/eval_jaxpr/all_gather | solution.py:99
  296.5 5.3 %collective-permute-start.1 = (f32[16,3,2,1024]{3,2,0,1:T(2,128)S(1)}, f32[16,3,2,1024]{3,2,0,1:T(2,128)}, u32[]{:S(2)}, u32[]{:S(2)}) collective-permute-start(f32[16,3,2,1024]{3,2,0,1:T(2,128)S(1)} %get-tuple-element.308), channel_id=1, source_target_pairs={{0,1},{1,2},{2,3},{4,5},{5,6},{6,7},{8,9},{9,10},{10,11},{12,13},{... | collective-permute-start | bytes 1179656 | tf_op jit(solution)/shard_map/while/body/eval_jaxpr/ppermute | solution.py:20
  304.5 9.6 %all-gather.2 = f32[1,3,12,1024]{3,2,1,0:T(8,128)S(1)} all-gather(f32[1,3,12,128]{3,2,1,0:T(8,128)S(1)} %constant_dynamic-slice_fusion.2), channel_id=2, replica_groups=mesh['mode'=8,'rows'=4] {'mode'}, dimensions={3}, use_global_device_ids=true | all-gather | bytes 165888 | tf_op jit(solution)/shard_map/while/body/eval_jaxpr/all_gather | solution.py:99
  334.9 7.4 %copy.42 = f32[16,3,8,1024]{0,2,1,3:T(8,128)} copy(f32[16,3,8,1024]{3,2,1,0:T(8,128)S(1)} %get-tuple-element.418) | data formatting | bytes 3145728 | tf_op jit(solution)/shard_map/while | solution.py:107
  342.3 9.8 %reshape.42 = f32[8,1,49152]{2,1,0:T(1,128)} reshape(f32[1024,3,8,16]{3,2,1,0:T(8,128)} %bitcast.127) | data formatting | bytes 3145728
  355.7 20.9 %all-to-all-done = f32[8,1,49152]{2,1,0:T(1,128)S(1)} async-done(((f32[8,1,49152]{2,1,0:T(1,128)}), f32[8,1,49152]{2,1,0:T(1,128)S(1)}, u32[]{:S(2)}, u32[]{:S(2)}) %all-to-all-start) | async-done | bytes 1572896 | tf_op jit(solution)/shard_map/all_to_all | solution.py:109
  381.5 8.7 %reshape.43 = f32[1024,3,8,16]{3,2,1,0:T(8,128)} reshape(f32[8,49152]{1,0:T(8,128)S(1)} %reduce) | data formatting | bytes 3145728
  390.2 7.5 %copy.43 = f32[16,3,8,8,128]{4,2,1,0,3:T(8,128)S(1)} copy(f32[16,3,8,8,128]{0,2,1,4,3:T(8,128)} %bitcast.128) | data formatting | bytes 3145728 | tf_op jit(solution)/shard_map/all_to_all | solution.py:109
  (546 shorter events, 203.2 us)
Async XLA Ops:
  1.0 17.8 %collective-permute-start.4 = (f32[8,3,2,128]{3,2,1,0:T(2,128)S(1)}, f32[8,3,2,128]{3,2,1,0:T(2,128)S(1)}, u32[]{:S(2)}, u32[]{:S(2)}) collective-permute-start(f32[8,3,2,128]{3,2,1,0:T(2,128)S(1)} %get-tuple-element.196), channel_id=1, source_target_pairs={{0,1},{1,2},{2,3},{4,5},{5,6},{6,7},{8,9},{9,10},{10,11},{12,13},{... | collective-permute-start | bytes 73736 | tf_op jit(solution)/shard_map/ppermute | solution.py:20
  6.0 12.8 %collective-permute-start.5 = (f32[8,3,2,128]{3,2,1,0:T(2,128)S(1)}, f32[8,3,2,128]{3,2,1,0:T(2,128)S(1)}, u32[]{:S(2)}, u32[]{:S(2)}) collective-permute-start(f32[8,3,2,128]{3,2,1,0:T(2,128)S(1)} %get-tuple-element.197), channel_id=1, source_target_pairs={{1,0},{2,1},{3,2},{5,4},{6,5},{7,6},{9,8},{10,9},{11,10},{13,12},{... | collective-permute-start | bytes 73736 | tf_op jit(solution)/shard_map/ppermute | solution.py:22
  8.0 7.5 %collective-permute-start.2 = (f32[1,1,2,1024]{3,2,1,0:T(2,128)S(1)}, f32[1,1,2,1024]{3,2,1,0:T(2,128)S(1)}, u32[]{:S(2)}, u32[]{:S(2)}) collective-permute-start(f32[1,1,2,1024]{3,2,1,0:T(2,128)S(1)} %get-tuple-element.198), channel_id=1, source_target_pairs={{0,1},{1,2},{2,3},{4,5},{5,6},{6,7},{8,9},{9,10},{10,11},{12,13},{... | collective-permute-start | bytes 24584 | tf_op jit(solution)/shard_map/ppermute | solution.py:20
  12.6 5.5 %collective-permute-start.3 = (f32[1,1,2,1024]{3,2,1,0:T(2,128)S(1)}, f32[1,1,2,1024]{3,2,1,0:T(2,128)S(1)}, u32[]{:S(2)}, u32[]{:S(2)}) collective-permute-start(f32[1,1,2,1024]{3,2,1,0:T(2,128)S(1)} %get-tuple-element.199), channel_id=1, source_target_pairs={{1,0},{2,1},{3,2},{5,4},{6,5},{7,6},{9,8},{10,9},{11,10},{13,12},{... | collective-permute-start | bytes 24584 | tf_op jit(solution)/shard_map/ppermute | solution.py:22
  18.9 20.7 %copy-start.6 = (f32[8,3,12,128]{3,2,1,0:T(8,128)}, f32[8,3,12,128]{3,2,1,0:T(8,128)S(1)}, u32[]{:S(2)}) copy-start(f32[8,3,12,128]{3,2,1,0:T(8,128)S(1)} %get-tuple-element.401) | copy-start | bytes 442372 | tf_op jit(solution)/shard_map/while
  19.2 24.3 %collective-permute-start = (f32[16,3,2,1024]{3,2,0,1:T(2,128)S(1)}, f32[16,3,2,1024]{3,2,0,1:T(2,128)S(1)}, u32[]{:S(2)}, u32[]{:S(2)}) collective-permute-start(f32[16,3,2,1024]{3,2,0,1:T(2,128)S(1)} %get-tuple-element.307), channel_id=1, source_target_pairs={{1,0},{2,1},{3,2},{5,4},{6,5},{7,6},{9,8},{10,9},{11,10},{13,12},{... | collective-permute-start | bytes 1179656 | tf_op jit(solution)/shard_map/while/body/eval_jaxpr/ppermute | solution.py:22
  20.5 23.0 %collective-permute-start.1 = (f32[16,3,2,1024]{3,2,0,1:T(2,128)S(1)}, f32[16,3,2,1024]{3,2,0,1:T(2,128)}, u32[]{:S(2)}, u32[]{:S(2)}) collective-permute-start(f32[16,3,2,1024]{3,2,0,1:T(2,128)S(1)} %get-tuple-element.308), channel_id=1, source_target_pairs={{0,1},{1,2},{2,3},{4,5},{5,6},{6,7},{8,9},{9,10},{10,11},{12,13},{... | collective-permute-start | bytes 1179656 | tf_op jit(solution)/shard_map/while/body/eval_jaxpr/ppermute | solution.py:20
  58.7 20.6 %copy-start.6 = (f32[8,3,12,128]{3,2,1,0:T(8,128)}, f32[8,3,12,128]{3,2,1,0:T(8,128)S(1)}, u32[]{:S(2)}) copy-start(f32[8,3,12,128]{3,2,1,0:T(8,128)S(1)} %get-tuple-element.401) | copy-start | bytes 442372 | tf_op jit(solution)/shard_map/while
  59.0 24.3 %collective-permute-start = (f32[16,3,2,1024]{3,2,0,1:T(2,128)S(1)}, f32[16,3,2,1024]{3,2,0,1:T(2,128)S(1)}, u32[]{:S(2)}, u32[]{:S(2)}) collective-permute-start(f32[16,3,2,1024]{3,2,0,1:T(2,128)S(1)} %get-tuple-element.307), channel_id=1, source_target_pairs={{1,0},{2,1},{3,2},{5,4},{6,5},{7,6},{9,8},{10,9},{11,10},{13,12},{... | collective-permute-start | bytes 1179656 | tf_op jit(solution)/shard_map/while/body/eval_jaxpr/ppermute | solution.py:22
  60.3 23.0 %collective-permute-start.1 = (f32[16,3,2,1024]{3,2,0,1:T(2,128)S(1)}, f32[16,3,2,1024]{3,2,0,1:T(2,128)}, u32[]{:S(2)}, u32[]{:S(2)}) collective-permute-start(f32[16,3,2,1024]{3,2,0,1:T(2,128)S(1)} %get-tuple-element.308), channel_id=1, source_target_pairs={{0,1},{1,2},{2,3},{4,5},{5,6},{6,7},{8,9},{9,10},{10,11},{12,13},{... | collective-permute-start | bytes 1179656 | tf_op jit(solution)/shard_map/while/body/eval_jaxpr/ppermute | solution.py:20
  98.9 23.4 %collective-permute-start = (f32[16,3,2,1024]{3,2,0,1:T(2,128)S(1)}, f32[16,3,2,1024]{3,2,0,1:T(2,128)S(1)}, u32[]{:S(2)}, u32[]{:S(2)}) collective-permute-start(f32[16,3,2,1024]{3,2,0,1:T(2,128)S(1)} %get-tuple-element.307), channel_id=1, source_target_pairs={{1,0},{2,1},{3,2},{5,4},{6,5},{7,6},{9,8},{10,9},{11,10},{13,12},{... | collective-permute-start | bytes 1179656 | tf_op jit(solution)/shard_map/while/body/eval_jaxpr/ppermute | solution.py:22
  100.2 22.1 %collective-permute-start.1 = (f32[16,3,2,1024]{3,2,0,1:T(2,128)S(1)}, f32[16,3,2,1024]{3,2,0,1:T(2,128)}, u32[]{:S(2)}, u32[]{:S(2)}) collective-permute-start(f32[16,3,2,1024]{3,2,0,1:T(2,128)S(1)} %get-tuple-element.308), channel_id=1, source_target_pairs={{0,1},{1,2},{2,3},{4,5},{5,6},{6,7},{8,9},{9,10},{10,11},{12,13},{... | collective-permute-start | bytes 1179656 | tf_op jit(solution)/shard_map/while/body/eval_jaxpr/ppermute | solution.py:20
  137.7 24.3 %collective-permute-start = (f32[16,3,2,1024]{3,2,0,1:T(2,128)S(1)}, f32[16,3,2,1024]{3,2,0,1:T(2,128)S(1)}, u32[]{:S(2)}, u32[]{:S(2)}) collective-permute-start(f32[16,3,2,1024]{3,2,0,1:T(2,128)S(1)} %get-tuple-element.307), channel_id=1, source_target_pairs={{1,0},{2,1},{3,2},{5,4},{6,5},{7,6},{9,8},{10,9},{11,10},{13,12},{... | collective-permute-start | bytes 1179656 | tf_op jit(solution)/shard_map/while/body/eval_jaxpr/ppermute | solution.py:22
  139.0 23.0 %collective-permute-start.1 = (f32[16,3,2,1024]{3,2,0,1:T(2,128)S(1)}, f32[16,3,2,1024]{3,2,0,1:T(2,128)}, u32[]{:S(2)}, u32[]{:S(2)}) collective-permute-start(f32[16,3,2,1024]{3,2,0,1:T(2,128)S(1)} %get-tuple-element.308), channel_id=1, source_target_pairs={{0,1},{1,2},{2,3},{4,5},{5,6},{6,7},{8,9},{9,10},{10,11},{12,13},{... | collective-permute-start | bytes 1179656 | tf_op jit(solution)/shard_map/while/body/eval_jaxpr/ppermute | solution.py:20
  177.6 23.4 %collective-permute-start = (f32[16,3,2,1024]{3,2,0,1:T(2,128)S(1)}, f32[16,3,2,1024]{3,2,0,1:T(2,128)S(1)}, u32[]{:S(2)}, u32[]{:S(2)}) collective-permute-start(f32[16,3,2,1024]{3,2,0,1:T(2,128)S(1)} %get-tuple-element.307), channel_id=1, source_target_pairs={{1,0},{2,1},{3,2},{5,4},{6,5},{7,6},{9,8},{10,9},{11,10},{13,12},{... | collective-permute-start | bytes 1179656 | tf_op jit(solution)/shard_map/while/body/eval_jaxpr/ppermute | solution.py:22
  178.9 22.1 %collective-permute-start.1 = (f32[16,3,2,1024]{3,2,0,1:T(2,128)S(1)}, f32[16,3,2,1024]{3,2,0,1:T(2,128)}, u32[]{:S(2)}, u32[]{:S(2)}) collective-permute-start(f32[16,3,2,1024]{3,2,0,1:T(2,128)S(1)} %get-tuple-element.308), channel_id=1, source_target_pairs={{0,1},{1,2},{2,3},{4,5},{5,6},{6,7},{8,9},{9,10},{10,11},{12,13},{... | collective-permute-start | bytes 1179656 | tf_op jit(solution)/shard_map/while/body/eval_jaxpr/ppermute | solution.py:20
  216.2 20.6 %copy-start.6 = (f32[8,3,12,128]{3,2,1,0:T(8,128)}, f32[8,3,12,128]{3,2,1,0:T(8,128)S(1)}, u32[]{:S(2)}) copy-start(f32[8,3,12,128]{3,2,1,0:T(8,128)S(1)} %get-tuple-element.401) | copy-start | bytes 442372 | tf_op jit(solution)/shard_map/while
  216.5 24.3 %collective-permute-start = (f32[16,3,2,1024]{3,2,0,1:T(2,128)S(1)}, f32[16,3,2,1024]{3,2,0,1:T(2,128)S(1)}, u32[]{:S(2)}, u32[]{:S(2)}) collective-permute-start(f32[16,3,2,1024]{3,2,0,1:T(2,128)S(1)} %get-tuple-element.307), channel_id=1, source_target_pairs={{1,0},{2,1},{3,2},{5,4},{6,5},{7,6},{9,8},{10,9},{11,10},{13,12},{... | collective-permute-start | bytes 1179656 | tf_op jit(solution)/shard_map/while/body/eval_jaxpr/ppermute | solution.py:22
  217.8 23.0 %collective-permute-start.1 = (f32[16,3,2,1024]{3,2,0,1:T(2,128)S(1)}, f32[16,3,2,1024]{3,2,0,1:T(2,128)}, u32[]{:S(2)}, u32[]{:S(2)}) collective-permute-start(f32[16,3,2,1024]{3,2,0,1:T(2,128)S(1)} %get-tuple-element.308), channel_id=1, source_target_pairs={{0,1},{1,2},{2,3},{4,5},{5,6},{6,7},{8,9},{9,10},{10,11},{12,13},{... | collective-permute-start | bytes 1179656 | tf_op jit(solution)/shard_map/while/body/eval_jaxpr/ppermute | solution.py:20
  256.3 23.4 %collective-permute-start = (f32[16,3,2,1024]{3,2,0,1:T(2,128)S(1)}, f32[16,3,2,1024]{3,2,0,1:T(2,128)S(1)}, u32[]{:S(2)}, u32[]{:S(2)}) collective-permute-start(f32[16,3,2,1024]{3,2,0,1:T(2,128)S(1)} %get-tuple-element.307), channel_id=1, source_target_pairs={{1,0},{2,1},{3,2},{5,4},{6,5},{7,6},{9,8},{10,9},{11,10},{13,12},{... | collective-permute-start | bytes 1179656 | tf_op jit(solution)/shard_map/while/body/eval_jaxpr/ppermute | solution.py:22
  257.6 22.1 %collective-permute-start.1 = (f32[16,3,2,1024]{3,2,0,1:T(2,128)S(1)}, f32[16,3,2,1024]{3,2,0,1:T(2,128)}, u32[]{:S(2)}, u32[]{:S(2)}) collective-permute-start(f32[16,3,2,1024]{3,2,0,1:T(2,128)S(1)} %get-tuple-element.308), channel_id=1, source_target_pairs={{0,1},{1,2},{2,3},{4,5},{5,6},{6,7},{8,9},{9,10},{10,11},{12,13},{... | collective-permute-start | bytes 1179656 | tf_op jit(solution)/shard_map/while/body/eval_jaxpr/ppermute | solution.py:20
  295.2 24.3 %collective-permute-start = (f32[16,3,2,1024]{3,2,0,1:T(2,128)S(1)}, f32[16,3,2,1024]{3,2,0,1:T(2,128)S(1)}, u32[]{:S(2)}, u32[]{:S(2)}) collective-permute-start(f32[16,3,2,1024]{3,2,0,1:T(2,128)S(1)} %get-tuple-element.307), channel_id=1, source_target_pairs={{1,0},{2,1},{3,2},{5,4},{6,5},{7,6},{9,8},{10,9},{11,10},{13,12},{... | collective-permute-start | bytes 1179656 | tf_op jit(solution)/shard_map/while/body/eval_jaxpr/ppermute | solution.py:22
  296.5 23.0 %collective-permute-start.1 = (f32[16,3,2,1024]{3,2,0,1:T(2,128)S(1)}, f32[16,3,2,1024]{3,2,0,1:T(2,128)}, u32[]{:S(2)}, u32[]{:S(2)}) collective-permute-start(f32[16,3,2,1024]{3,2,0,1:T(2,128)S(1)} %get-tuple-element.308), channel_id=1, source_target_pairs={{0,1},{1,2},{2,3},{4,5},{5,6},{6,7},{8,9},{9,10},{10,11},{12,13},{... | collective-permute-start | bytes 1179656 | tf_op jit(solution)/shard_map/while/body/eval_jaxpr/ppermute | solution.py:20
  352.1 24.5 %all-to-all-start = ((f32[8,1,49152]{2,1,0:T(1,128)}), f32[8,1,49152]{2,1,0:T(1,128)S(1)}, u32[]{:S(2)}, u32[]{:S(2)}) async-start(f32[8,1,49152]{2,1,0:T(1,128)} %reshape.42), calls=%async_computation | async-start | bytes 3145728 | tf_op jit(solution)/shard_map/all_to_all | solution.py:109
  (72 other events, 195.3 us)
where the time goes:
time: 406 us; the launch traced here: 402 us
  other arithmetic  119 us (29%)
  local copies, waits for them, and re-layouts  97 us (24%)
  blocking collectives  73.6 us (18%)
  starting transfers between devices  68.4 us (17%)
  waiting for transfers between devices  23.5 us (6%)
  loops' own time  19.3 us (5%)
    all_gather x8, blocking collectives, fetch_flow(): return lax.all_gather(held_tile, 'mode', axis=2, tiled=True)  73.6 us
    another operation x56, other arithmetic, tendency(): return jnp.stack([height_rate, zonal_rate, merid_rate], 1)  53.8 us
    ppermute x10, starting transfers between devices, padded(): lax.ppermute(tail, axis, [(i, (i + 1) % count) for i in range(ends)])  51.9 us
    slice x144, local copies, waits for them, and re-layouts, deriv_x(): return 0.5 * (jnp.roll(values, -1, -1) - jnp.roll(values, 1, -1))  37.2 us
    mul x32, other arithmetic, deriv_x(): return 0.5 * (jnp.roll(values, -1, -1) - jnp.roll(values, 1, -1))  24.6 us
    all_to_all x1, waiting for transfers between devices, on_device(): lax.all_to_all(final, 'mode', split_axis=3, concat_axis=0, tiled=True)  20.9 us
    another operation x1, loops' own time, on_device(): final = lax.fori_loop(0, total_steps, advance, current)  19.3 us
    unnamed x8, local copies, waits for them, and re-layouts  18.9 us
  transfers between devices with their start and end apart: 21, of which 2 were waited for; matrix products, arithmetic and copies ran while one was open for 13% of the time, Pallas kernels for 0%

commit v1 on v0

--- a/solution.py
+++ b/solution.py
@@ -106,7 +106,13 @@
 
     final = lax.fori_loop(0, total_steps, advance, current)
     mixing = jnp.eye(coefficients.shape[0], dtype=jnp.float32) + jnp.triu(coefficients)
-    cell_block = lax.all_to_all(final, "mode", split_axis=3, concat_axis=0, tiled=True)
+    detail_lane = lambda inp, device_axis: jnp.concatenate(
+        jax.lax.all_to_all(
+            jnp.stack(jnp.split(inp, jax.lax.axis_size(device_axis), axis=3)), device_axis, 0, 0
+        ),
+        axis=0,
+    )
+    cell_block = detail_lane(final, "mode")
     flattened = cell_block.reshape(cell_block.shape[0], -1)
     mixed = jnp.dot(
         mixing.T, flattened, precision=lax.Precision.HIGHEST, preferred_element_type=jnp.float32

time: 406 us -> 373 us (0.919)
  local copies, waits for them, and re-layouts: 97 us -> 68.9 us
  other arithmetic: 119 us -> 114 us
    unnamed x8 -> x13, local copies, waits for them, and re-layouts: 18.9 us -> 5.3 us
    all_to_all x2 -> x0, local copies, waits for them, and re-layouts: 7.99 us -> none  [on_device(): lax.all_to_all(final, 'mode', split_axis=3, concat_axis=0, tiled=True)]
    while x145 -> x144, local copies, waits for them, and re-layouts: 12.7 us -> 5.34 us  [the longest x1 7.37 us: on_device(): final = lax.fori_loop(0, total_steps, advance, current)]
    all_to_all x1 -> x0, other arithmetic: 4.38 us -> none  [on_device(): lax.all_to_all(final, 'mode', split_axis=3, concat_axis=0, tiled=True)]
  transfers between devices with their start and end apart: 21 -> 21, of which waited for: 2 -> 2; matrix products, arithmetic and copies ran while one was open for 13% -> 14% of each run, Pallas kernels for 0% -> 0%
where the time goes in v1:
time: 373 us; the launch traced here: 370 us
  other arithmetic  114 us (31%)
  blocking collectives  73.6 us (20%)
  local copies, waits for them, and re-layouts  68.9 us (18%)
  starting transfers between devices  68.3 us (18%)
  waiting for transfers between devices  23.5 us (6%)
  loops' own time  19.3 us (5%)
    all_gather x8, blocking collectives, fetch_flow(): return lax.all_gather(held_tile, 'mode', axis=2, tiled=True)  73.6 us
    another operation x56, other arithmetic, tendency(): return jnp.stack([height_rate, zonal_rate, merid_rate], 1)  53.8 us
    ppermute x10, starting transfers between devices, padded(): lax.ppermute(tail, axis, [(i, (i + 1) % count) for i in range(ends)])  51.8 us
    slice x144, local copies, waits for them, and re-layouts, deriv_x(): return 0.5 * (jnp.roll(values, -1, -1) - jnp.roll(values, 1, -1))  37.3 us
    mul x32, other arithmetic, deriv_x(): return 0.5 * (jnp.roll(values, -1, -1) - jnp.roll(values, 1, -1))  24.6 us
    all_to_all x1, waiting for transfers between devices, on_device(): jax.lax.all_to_all(jnp.stack(jnp.split(inp, jax.lax.axis_size(device_axis...  20.9 us
    another operation x1, loops' own time, on_device(): final = lax.fori_loop(0, total_steps, advance, current)  19.3 us
    ppermute x10, starting transfers between devices, padded(): lax.ppermute(head, axis, [((i + 1) % count, i) for i in range(ends)])  12.9 us
  transfers between devices with their start and end apart: 21, of which 2 were waited for; matrix products, arithmetic and copies ran while one was open for 14% of the time, Pallas kernels for 0%

profile of v1, /device:TPU:0, one launch (start us, length us, event | category | flops | bytes accessed | tf_op | source)
XLA Modules:
  0.0 369.8 jit_solution(5539356471445465971)
XLA Ops:
  1.0 5.0 %collective-permute-start.4 = (f32[8,3,2,128]{3,2,1,0:T(2,128)S(1)}, f32[8,3,2,128]{3,2,1,0:T(2,128)S(1)}, u32[]{:S(2)}, u32[]{:S(2)}) collective-permute-start(f32[8,3,2,128]{3,2,1,0:T(2,128)S(1)} %get-tuple-element.196), channel_id=1, source_target_pairs={{0,1},{1,2},{2,3},{4,5},{5,6},{6,7},{8,9},{9,10},{10,11},{12,13},{... | collective-permute-start | bytes 73736 | tf_op jit(solution)/shard_map/ppermute | solution.py:20
  8.0 4.5 %collective-permute-start.2 = (f32[1,1,2,1024]{3,2,1,0:T(2,128)S(1)}, f32[1,1,2,1024]{3,2,1,0:T(2,128)S(1)}, u32[]{:S(2)}, u32[]{:S(2)}) collective-permute-start(f32[1,1,2,1024]{3,2,1,0:T(2,128)S(1)} %get-tuple-element.198), channel_id=1, source_target_pairs={{0,1},{1,2},{2,3},{4,5},{5,6},{6,7},{8,9},{9,10},{10,11},{12,13},{... | collective-permute-start | bytes 24584 | tf_op jit(solution)/shard_map/ppermute | solution.py:20
  13.9 1.6 broadcast_multiply_fusion.1
  15.6 2.6 collective-permute-done.3
  18.8 316.1 %while.13 = (s32[]{:T(128)}, f32[16,3,8,1024]{3,2,1,0:T(8,128)S(1)}, f32[12,1024]{1,0:T(8,128)}, s32[8]{0:T(128)S(1)}, f32[8,3,12,128]{3,2,1,0:T(8,128)S(1)}, /*...) while((s32[]{:T(128)}, f32[16,3,8,1024]{3,2,1,0:T(8,128)S(1)}, f32[12,1024]{1,0:T(8,128)}, s32[8]{0:T(128)S(1)}, ...), condition=%wide.region_1.2_spmd, body=%wide.region_0.1_spmd.sunk | while | flops 21987332 | bytes 97589864 | solution.py:107
  20.5 5.3 %collective-permute-start.1 = (f32[16,3,2,1024]{3,2,0,1:T(2,128)S(1)}, f32[16,3,2,1024]{3,2,0,1:T(2,128)}, u32[]{:S(2)}, u32[]{:S(2)}) collective-permute-start(f32[16,3,2,1024]{3,2,0,1:T(2,128)S(1)} %get-tuple-element.308), channel_id=1, source_target_pairs={{0,1},{1,2},{2,3},{4,5},{5,6},{6,7},{8,9},{9,10},{10,11},{12,13},{... | collective-permute-start | bytes 1179656 | tf_op jit(solution)/shard_map/while/body/eval_jaxpr/ppermute | solution.py:20
  28.5 9.6 %all-gather.2 = f32[1,3,12,1024]{3,2,1,0:T(8,128)S(1)} all-gather(f32[1,3,12,128]{3,2,1,0:T(8,128)S(1)} %constant_dynamic-slice_fusion.2), channel_id=2, replica_groups=mesh['mode'=8,'rows'=4] {'mode'}, dimensions={3}, use_global_device_ids=true | all-gather | bytes 165888 | tf_op jit(solution)/shard_map/while/body/eval_jaxpr/all_gather | solution.py:99
  60.3 5.3 %collective-permute-start.1 = (f32[16,3,2,1024]{3,2,0,1:T(2,128)S(1)}, f32[16,3,2,1024]{3,2,0,1:T(2,128)}, u32[]{:S(2)}, u32[]{:S(2)}) collective-permute-start(f32[16,3,2,1024]{3,2,0,1:T(2,128)S(1)} %get-tuple-element.308), channel_id=1, source_target_pairs={{0,1},{1,2},{2,3},{4,5},{5,6},{6,7},{8,9},{9,10},{10,11},{12,13},{... | collective-permute-start | bytes 1179656 | tf_op jit(solution)/shard_map/while/body/eval_jaxpr/ppermute | solution.py:20
  68.4 9.6 %all-gather.2 = f32[1,3,12,1024]{3,2,1,0:T(8,128)S(1)} all-gather(f32[1,3,12,128]{3,2,1,0:T(8,128)S(1)} %constant_dynamic-slice_fusion.2), channel_id=2, replica_groups=mesh['mode'=8,'rows'=4] {'mode'}, dimensions={3}, use_global_device_ids=true | all-gather | bytes 165888 | tf_op jit(solution)/shard_map/while/body/eval_jaxpr/all_gather | solution.py:99
  100.2 5.3 %collective-permute-start.1 = (f32[16,3,2,1024]{3,2,0,1:T(2,128)S(1)}, f32[16,3,2,1024]{3,2,0,1:T(2,128)}, u32[]{:S(2)}, u32[]{:S(2)}) collective-permute-start(f32[16,3,2,1024]{3,2,0,1:T(2,128)S(1)} %get-tuple-element.308), channel_id=1, source_target_pairs={{0,1},{1,2},{2,3},{4,5},{5,6},{6,7},{8,9},{9,10},{10,11},{12,13},{... | collective-permute-start | bytes 1179656 | tf_op jit(solution)/shard_map/while/body/eval_jaxpr/ppermute | solution.py:20
  108.2 8.6 %all-gather.2 = f32[1,3,12,1024]{3,2,1,0:T(8,128)S(1)} all-gather(f32[1,3,12,128]{3,2,1,0:T(8,128)S(1)} %constant_dynamic-slice_fusion.2), channel_id=2, replica_groups=mesh['mode'=8,'rows'=4] {'mode'}, dimensions={3}, use_global_device_ids=true | all-gather | bytes 165888 | tf_op jit(solution)/shard_map/while/body/eval_jaxpr/all_gather | solution.py:99
  139.1 5.3 %collective-permute-start.1 = (f32[16,3,2,1024]{3,2,0,1:T(2,128)S(1)}, f32[16,3,2,1024]{3,2,0,1:T(2,128)}, u32[]{:S(2)}, u32[]{:S(2)}) collective-permute-start(f32[16,3,2,1024]{3,2,0,1:T(2,128)S(1)} %get-tuple-element.308), channel_id=1, source_target_pairs={{0,1},{1,2},{2,3},{4,5},{5,6},{6,7},{8,9},{9,10},{10,11},{12,13},{... | collective-permute-start | bytes 1179656 | tf_op jit(solution)/shard_map/while/body/eval_jaxpr/ppermute | solution.py:20
  147.1 9.6 %all-gather.2 = f32[1,3,12,1024]{3,2,1,0:T(8,128)S(1)} all-gather(f32[1,3,12,128]{3,2,1,0:T(8,128)S(1)} %constant_dynamic-slice_fusion.2), channel_id=2, replica_groups=mesh['mode'=8,'rows'=4] {'mode'}, dimensions={3}, use_global_device_ids=true | all-gather | bytes 165888 | tf_op jit(solution)/shard_map/while/body/eval_jaxpr/all_gather | solution.py:99
  178.9 5.3 %collective-permute-start.1 = (f32[16,3,2,1024]{3,2,0,1:T(2,128)S(1)}, f32[16,3,2,1024]{3,2,0,1:T(2,128)}, u32[]{:S(2)}, u32[]{:S(2)}) collective-permute-start(f32[16,3,2,1024]{3,2,0,1:T(2,128)S(1)} %get-tuple-element.308), channel_id=1, source_target_pairs={{0,1},{1,2},{2,3},{4,5},{5,6},{6,7},{8,9},{9,10},{10,11},{12,13},{... | collective-permute-start | bytes 1179656 | tf_op jit(solution)/shard_map/while/body/eval_jaxpr/ppermute | solution.py:20
  187.0 8.6 %all-gather.2 = f32[1,3,12,1024]{3,2,1,0:T(8,128)S(1)} all-gather(f32[1,3,12,128]{3,2,1,0:T(8,128)S(1)} %constant_dynamic-slice_fusion.2), channel_id=2, replica_groups=mesh['mode'=8,'rows'=4] {'mode'}, dimensions={3}, use_global_device_ids=true | all-gather | bytes 165888 | tf_op jit(solution)/shard_map/while/body/eval_jaxpr/all_gather | solution.py:99
  217.8 5.3 %collective-permute-start.1 = (f32[16,3,2,1024]{3,2,0,1:T(2,128)S(1)}, f32[16,3,2,1024]{3,2,0,1:T(2,128)}, u32[]{:S(2)}, u32[]{:S(2)}) collective-permute-start(f32[16,3,2,1024]{3,2,0,1:T(2,128)S(1)} %get-tuple-element.308), channel_id=1, source_target_pairs={{0,1},{1,2},{2,3},{4,5},{5,6},{6,7},{8,9},{9,10},{10,11},{12,13},{... | collective-permute-start | bytes 1179656 | tf_op jit(solution)/shard_map/while/body/eval_jaxpr/ppermute | solution.py:20
  225.8 9.6 %all-gather.2 = f32[1,3,12,1024]{3,2,1,0:T(8,128)S(1)} all-gather(f32[1,3,12,128]{3,2,1,0:T(8,128)S(1)} %constant_dynamic-slice_fusion.2), channel_id=2, replica_groups=mesh['mode'=8,'rows'=4] {'mode'}, dimensions={3}, use_global_device_ids=true | all-gather | bytes 165888 | tf_op jit(solution)/shard_map/while/body/eval_jaxpr/all_gather | solution.py:99
  257.6 5.3 %collective-permute-start.1 = (f32[16,3,2,1024]{3,2,0,1:T(2,128)S(1)}, f32[16,3,2,1024]{3,2,0,1:T(2,128)}, u32[]{:S(2)}, u32[]{:S(2)}) collective-permute-start(f32[16,3,2,1024]{3,2,0,1:T(2,128)S(1)} %get-tuple-element.308), channel_id=1, source_target_pairs={{0,1},{1,2},{2,3},{4,5},{5,6},{6,7},{8,9},{9,10},{10,11},{12,13},{... | collective-permute-start | bytes 1179656 | tf_op jit(solution)/shard_map/while/body/eval_jaxpr/ppermute | solution.py:20
  265.7 8.6 %all-gather.2 = f32[1,3,12,1024]{3,2,1,0:T(8,128)S(1)} all-gather(f32[1,3,12,128]{3,2,1,0:T(8,128)S(1)} %constant_dynamic-slice_fusion.2), channel_id=2, replica_groups=mesh['mode'=8,'rows'=4] {'mode'}, dimensions={3}, use_global_device_ids=true | all-gather | bytes 165888 | tf_op jit(solution)/shard_map/while/body/eval_jaxpr/all_gather | solution.py:99
  296.5 5.3 %collective-permute-start.1 = (f32[16,3,2,1024]{3,2,0,1:T(2,128)S(1)}, f32[16,3,2,1024]{3,2,0,1:T(2,128)}, u32[]{:S(2)}, u32[]{:S(2)}) collective-permute-start(f32[16,3,2,1024]{3,2,0,1:T(2,128)S(1)} %get-tuple-element.308), channel_id=1, source_target_pairs={{0,1},{1,2},{2,3},{4,5},{5,6},{6,7},{8,9},{9,10},{10,11},{12,13},{... | collective-permute-start | bytes 1179656 | tf_op jit(solution)/shard_map/while/body/eval_jaxpr/ppermute | solution.py:20
  304.6 9.6 %all-gather.2 = f32[1,3,12,1024]{3,2,1,0:T(8,128)S(1)} all-gather(f32[1,3,12,128]{3,2,1,0:T(8,128)S(1)} %constant_dynamic-slice_fusion.2), channel_id=2, replica_groups=mesh['mode'=8,'rows'=4] {'mode'}, dimensions={3}, use_global_device_ids=true | all-gather | bytes 165888 | tf_op jit(solution)/shard_map/while/body/eval_jaxpr/all_gather | solution.py:99
  340.6 3.6 all-to-all-start
  344.2 20.9 %all-to-all-done = f32[8,16,3,8,128]{4,3,2,1,0:T(8,128)S(1)} async-done(((f32[8,16,3,8,128]{4,3,2,1,0:T(8,128)}), f32[8,16,3,8,128]{4,3,2,1,0:T(8,128)S(1)}, u32[]{:S(2)}, u32[]{:S(2)}) %all-to-all-start) | async-done | bytes 1572896 | tf_op jit(solution)/shard_map/all_to_all | solution.py:110
  367.7 2.1 copy.14
  (548 shorter events, 194.1 us)
Async XLA Ops:
  1.0 17.8 %collective-permute-start.4 = (f32[8,3,2,128]{3,2,1,0:T(2,128)S(1)}, f32[8,3,2,128]{3,2,1,0:T(2,128)S(1)}, u32[]{:S(2)}, u32[]{:S(2)}) collective-permute-start(f32[8,3,2,128]{3,2,1,0:T(2,128)S(1)} %get-tuple-element.196), channel_id=1, source_target_pairs={{0,1},{1,2},{2,3},{4,5},{5,6},{6,7},{8,9},{9,10},{10,11},{12,13},{... | collective-permute-start | bytes 73736 | tf_op jit(solution)/shard_map/ppermute | solution.py:20
  6.0 12.8 %collective-permute-start.5 = (f32[8,3,2,128]{3,2,1,0:T(2,128)S(1)}, f32[8,3,2,128]{3,2,1,0:T(2,128)S(1)}, u32[]{:S(2)}, u32[]{:S(2)}) collective-permute-start(f32[8,3,2,128]{3,2,1,0:T(2,128)S(1)} %get-tuple-element.197), channel_id=1, source_target_pairs={{1,0},{2,1},{3,2},{5,4},{6,5},{7,6},{9,8},{10,9},{11,10},{13,12},{... | collective-permute-start | bytes 73736 | tf_op jit(solution)/shard_map/ppermute | solution.py:22
  8.0 7.5 %collective-permute-start.2 = (f32[1,1,2,1024]{3,2,1,0:T(2,128)S(1)}, f32[1,1,2,1024]{3,2,1,0:T(2,128)S(1)}, u32[]{:S(2)}, u32[]{:S(2)}) collective-permute-start(f32[1,1,2,1024]{3,2,1,0:T(2,128)S(1)} %get-tuple-element.198), channel_id=1, source_target_pairs={{0,1},{1,2},{2,3},{4,5},{5,6},{6,7},{8,9},{9,10},{10,11},{12,13},{... | collective-permute-start | bytes 24584 | tf_op jit(solution)/shard_map/ppermute | solution.py:20
  12.6 5.5 %collective-permute-start.3 = (f32[1,1,2,1024]{3,2,1,0:T(2,128)S(1)}, f32[1,1,2,1024]{3,2,1,0:T(2,128)S(1)}, u32[]{:S(2)}, u32[]{:S(2)}) collective-permute-start(f32[1,1,2,1024]{3,2,1,0:T(2,128)S(1)} %get-tuple-element.199), channel_id=1, source_target_pairs={{1,0},{2,1},{3,2},{5,4},{6,5},{7,6},{9,8},{10,9},{11,10},{13,12},{... | collective-permute-start | bytes 24584 | tf_op jit(solution)/shard_map/ppermute | solution.py:22
  18.9 20.7 %copy-start.6 = (f32[8,3,12,128]{3,2,1,0:T(8,128)}, f32[8,3,12,128]{3,2,1,0:T(8,128)S(1)}, u32[]{:S(2)}) copy-start(f32[8,3,12,128]{3,2,1,0:T(8,128)S(1)} %get-tuple-element.401) | copy-start | bytes 442372 | tf_op jit(solution)/shard_map/while
  19.2 24.3 %collective-permute-start = (f32[16,3,2,1024]{3,2,0,1:T(2,128)S(1)}, f32[16,3,2,1024]{3,2,0,1:T(2,128)S(1)}, u32[]{:S(2)}, u32[]{:S(2)}) collective-permute-start(f32[16,3,2,1024]{3,2,0,1:T(2,128)S(1)} %get-tuple-element.307), channel_id=1, source_target_pairs={{1,0},{2,1},{3,2},{5,4},{6,5},{7,6},{9,8},{10,9},{11,10},{13,12},{... | collective-permute-start | bytes 1179656 | tf_op jit(solution)/shard_map/while/body/eval_jaxpr/ppermute | solution.py:22
  20.5 23.1 %collective-permute-start.1 = (f32[16,3,2,1024]{3,2,0,1:T(2,128)S(1)}, f32[16,3,2,1024]{3,2,0,1:T(2,128)}, u32[]{:S(2)}, u32[]{:S(2)}) collective-permute-start(f32[16,3,2,1024]{3,2,0,1:T(2,128)S(1)} %get-tuple-element.308), channel_id=1, source_target_pairs={{0,1},{1,2},{2,3},{4,5},{5,6},{6,7},{8,9},{9,10},{10,11},{12,13},{... | collective-permute-start | bytes 1179656 | tf_op jit(solution)/shard_map/while/body/eval_jaxpr/ppermute | solution.py:20
  58.7 20.6 %copy-start.6 = (f32[8,3,12,128]{3,2,1,0:T(8,128)}, f32[8,3,12,128]{3,2,1,0:T(8,128)S(1)}, u32[]{:S(2)}) copy-start(f32[8,3,12,128]{3,2,1,0:T(8,128)S(1)} %get-tuple-element.401) | copy-start | bytes 442372 | tf_op jit(solution)/shard_map/while
  59.0 24.3 %collective-permute-start = (f32[16,3,2,1024]{3,2,0,1:T(2,128)S(1)}, f32[16,3,2,1024]{3,2,0,1:T(2,128)S(1)}, u32[]{:S(2)}, u32[]{:S(2)}) collective-permute-start(f32[16,3,2,1024]{3,2,0,1:T(2,128)S(1)} %get-tuple-element.307), channel_id=1, source_target_pairs={{1,0},{2,1},{3,2},{5,4},{6,5},{7,6},{9,8},{10,9},{11,10},{13,12},{... | collective-permute-start | bytes 1179656 | tf_op jit(solution)/shard_map/while/body/eval_jaxpr/ppermute | solution.py:22
  60.3 23.0 %collective-permute-start.1 = (f32[16,3,2,1024]{3,2,0,1:T(2,128)S(1)}, f32[16,3,2,1024]{3,2,0,1:T(2,128)}, u32[]{:S(2)}, u32[]{:S(2)}) collective-permute-start(f32[16,3,2,1024]{3,2,0,1:T(2,128)S(1)} %get-tuple-element.308), channel_id=1, source_target_pairs={{0,1},{1,2},{2,3},{4,5},{5,6},{6,7},{8,9},{9,10},{10,11},{12,13},{... | collective-permute-start | bytes 1179656 | tf_op jit(solution)/shard_map/while/body/eval_jaxpr/ppermute | solution.py:20
  98.9 23.4 %collective-permute-start = (f32[16,3,2,1024]{3,2,0,1:T(2,128)S(1)}, f32[16,3,2,1024]{3,2,0,1:T(2,128)S(1)}, u32[]{:S(2)}, u32[]{:S(2)}) collective-permute-start(f32[16,3,2,1024]{3,2,0,1:T(2,128)S(1)} %get-tuple-element.307), channel_id=1, source_target_pairs={{1,0},{2,1},{3,2},{5,4},{6,5},{7,6},{9,8},{10,9},{11,10},{13,12},{... | collective-permute-start | bytes 1179656 | tf_op jit(solution)/shard_map/while/body/eval_jaxpr/ppermute | solution.py:22
  100.2 22.1 %collective-permute-start.1 = (f32[16,3,2,1024]{3,2,0,1:T(2,128)S(1)}, f32[16,3,2,1024]{3,2,0,1:T(2,128)}, u32[]{:S(2)}, u32[]{:S(2)}) collective-permute-start(f32[16,3,2,1024]{3,2,0,1:T(2,128)S(1)} %get-tuple-element.308), channel_id=1, source_target_pairs={{0,1},{1,2},{2,3},{4,5},{5,6},{6,7},{8,9},{9,10},{10,11},{12,13},{... | collective-permute-start | bytes 1179656 | tf_op jit(solution)/shard_map/while/body/eval_jaxpr/ppermute | solution.py:20
  137.5 20.6 %copy-start.6 = (f32[8,3,12,128]{3,2,1,0:T(8,128)}, f32[8,3,12,128]{3,2,1,0:T(8,128)S(1)}, u32[]{:S(2)}) copy-start(f32[8,3,12,128]{3,2,1,0:T(8,128)S(1)} %get-tuple-element.401) | copy-start | bytes 442372 | tf_op jit(solution)/shard_map/while
  137.8 24.3 %collective-permute-start = (f32[16,3,2,1024]{3,2,0,1:T(2,128)S(1)}, f32[16,3,2,1024]{3,2,0,1:T(2,128)S(1)}, u32[]{:S(2)}, u32[]{:S(2)}) collective-permute-start(f32[16,3,2,1024]{3,2,0,1:T(2,128)S(1)} %get-tuple-element.307), channel_id=1, source_target_pairs={{1,0},{2,1},{3,2},{5,4},{6,5},{7,6},{9,8},{10,9},{11,10},{13,12},{... | collective-permute-start | bytes 1179656 | tf_op jit(solution)/shard_map/while/body/eval_jaxpr/ppermute | solution.py:22
  139.1 23.0 %collective-permute-start.1 = (f32[16,3,2,1024]{3,2,0,1:T(2,128)S(1)}, f32[16,3,2,1024]{3,2,0,1:T(2,128)}, u32[]{:S(2)}, u32[]{:S(2)}) collective-permute-start(f32[16,3,2,1024]{3,2,0,1:T(2,128)S(1)} %get-tuple-element.308), channel_id=1, source_target_pairs={{0,1},{1,2},{2,3},{4,5},{5,6},{6,7},{8,9},{9,10},{10,11},{12,13},{... | collective-permute-start | bytes 1179656 | tf_op jit(solution)/shard_map/while/body/eval_jaxpr/ppermute | solution.py:20
  177.6 23.4 %collective-permute-start = (f32[16,3,2,1024]{3,2,0,1:T(2,128)S(1)}, f32[16,3,2,1024]{3,2,0,1:T(2,128)S(1)}, u32[]{:S(2)}, u32[]{:S(2)}) collective-permute-start(f32[16,3,2,1024]{3,2,0,1:T(2,128)S(1)} %get-tuple-element.307), channel_id=1, source_target_pairs={{1,0},{2,1},{3,2},{5,4},{6,5},{7,6},{9,8},{10,9},{11,10},{13,12},{... | collective-permute-start | bytes 1179656 | tf_op jit(solution)/shard_map/while/body/eval_jaxpr/ppermute | solution.py:22
  178.9 22.1 %collective-permute-start.1 = (f32[16,3,2,1024]{3,2,0,1:T(2,128)S(1)}, f32[16,3,2,1024]{3,2,0,1:T(2,128)}, u32[]{:S(2)}, u32[]{:S(2)}) collective-permute-start(f32[16,3,2,1024]{3,2,0,1:T(2,128)S(1)} %get-tuple-element.308), channel_id=1, source_target_pairs={{0,1},{1,2},{2,3},{4,5},{5,6},{6,7},{8,9},{9,10},{10,11},{12,13},{... | collective-permute-start | bytes 1179656 | tf_op jit(solution)/shard_map/while/body/eval_jaxpr/ppermute | solution.py:20
  216.5 24.3 %collective-permute-start = (f32[16,3,2,1024]{3,2,0,1:T(2,128)S(1)}, f32[16,3,2,1024]{3,2,0,1:T(2,128)S(1)}, u32[]{:S(2)}, u32[]{:S(2)}) collective-permute-start(f32[16,3,2,1024]{3,2,0,1:T(2,128)S(1)} %get-tuple-element.307), channel_id=1, source_target_pairs={{1,0},{2,1},{3,2},{5,4},{6,5},{7,6},{9,8},{10,9},{11,10},{13,12},{... | collective-permute-start | bytes 1179656 | tf_op jit(solution)/shard_map/while/body/eval_jaxpr/ppermute | solution.py:22
  217.8 23.0 %collective-permute-start.1 = (f32[16,3,2,1024]{3,2,0,1:T(2,128)S(1)}, f32[16,3,2,1024]{3,2,0,1:T(2,128)}, u32[]{:S(2)}, u32[]{:S(2)}) collective-permute-start(f32[16,3,2,1024]{3,2,0,1:T(2,128)S(1)} %get-tuple-element.308), channel_id=1, source_target_pairs={{0,1},{1,2},{2,3},{4,5},{5,6},{6,7},{8,9},{9,10},{10,11},{12,13},{... | collective-permute-start | bytes 1179656 | tf_op jit(solution)/shard_map/while/body/eval_jaxpr/ppermute | solution.py:20
  256.3 23.4 %collective-permute-start = (f32[16,3,2,1024]{3,2,0,1:T(2,128)S(1)}, f32[16,3,2,1024]{3,2,0,1:T(2,128)S(1)}, u32[]{:S(2)}, u32[]{:S(2)}) collective-permute-start(f32[16,3,2,1024]{3,2,0,1:T(2,128)S(1)} %get-tuple-element.307), channel_id=1, source_target_pairs={{1,0},{2,1},{3,2},{5,4},{6,5},{7,6},{9,8},{10,9},{11,10},{13,12},{... | collective-permute-start | bytes 1179656 | tf_op jit(solution)/shard_map/while/body/eval_jaxpr/ppermute | solution.py:22
  257.6 22.1 %collective-permute-start.1 = (f32[16,3,2,1024]{3,2,0,1:T(2,128)S(1)}, f32[16,3,2,1024]{3,2,0,1:T(2,128)}, u32[]{:S(2)}, u32[]{:S(2)}) collective-permute-start(f32[16,3,2,1024]{3,2,0,1:T(2,128)S(1)} %get-tuple-element.308), channel_id=1, source_target_pairs={{0,1},{1,2},{2,3},{4,5},{5,6},{6,7},{8,9},{9,10},{10,11},{12,13},{... | collective-permute-start | bytes 1179656 | tf_op jit(solution)/shard_map/while/body/eval_jaxpr/ppermute | solution.py:20
  295.2 24.3 %collective-permute-start = (f32[16,3,2,1024]{3,2,0,1:T(2,128)S(1)}, f32[16,3,2,1024]{3,2,0,1:T(2,128)S(1)}, u32[]{:S(2)}, u32[]{:S(2)}) collective-permute-start(f32[16,3,2,1024]{3,2,0,1:T(2,128)S(1)} %get-tuple-element.307), channel_id=1, source_target_pairs={{1,0},{2,1},{3,2},{5,4},{6,5},{7,6},{9,8},{10,9},{11,10},{13,12},{... | collective-permute-start | bytes 1179656 | tf_op jit(solution)/shard_map/while/body/eval_jaxpr/ppermute | solution.py:22
  296.5 23.0 %collective-permute-start.1 = (f32[16,3,2,1024]{3,2,0,1:T(2,128)S(1)}, f32[16,3,2,1024]{3,2,0,1:T(2,128)}, u32[]{:S(2)}, u32[]{:S(2)}) collective-permute-start(f32[16,3,2,1024]{3,2,0,1:T(2,128)S(1)} %get-tuple-element.308), channel_id=1, source_target_pairs={{0,1},{1,2},{2,3},{4,5},{5,6},{6,7},{8,9},{9,10},{10,11},{12,13},{... | collective-permute-start | bytes 1179656 | tf_op jit(solution)/shard_map/while/body/eval_jaxpr/ppermute | solution.py:20
  340.6 24.5 %all-to-all-start = ((f32[8,16,3,8,128]{4,3,2,1,0:T(8,128)}), f32[8,16,3,8,128]{4,3,2,1,0:T(8,128)S(1)}, u32[]{:S(2)}, u32[]{:S(2)}) async-start(f32[8,16,3,8,128]{4,3,2,1,0:T(8,128)} %bitcast_dynamic-update-slice_fusion), calls=%async_computation | async-start | bytes 3145728 | tf_op jit(solution)/shard_map/all_to_all | solution.py:110
  (72 other events, 195.3 us)
